TPU v7x, 32 devices: a whole 2x2x4 slice. The times are simulated.
32 devices in a mesh: fsdp: 8 (over z, x), seq: 4 (over y, core).
Axes of the slice: x: 2, y: 2, z: 4, core: 2. Of those that a mesh axis runs over, the one named last changes fastest.
Arguments:
- context: bfloat16 [16, 512, 2560], P('fsdp', 'seq'), may hold values from -6 to 6
- residual: bfloat16 [16, 512, 2560], P('fsdp', 'seq'), may hold values from -6 to 6
- target_rows: bfloat16 [16, 512, 2560], P('fsdp', 'seq'), may hold values from -0.00390625 to 0.00390625
- log_norm: float32 [16, 512], P('fsdp', 'seq'), may hold values from -0.15 to 0.15
- norm_gain: float32 [2560], replicated, may hold values from 0.1 to 1.9
- out_proj: bfloat16 [2560, 2560], P('fsdp'), may hold values from -0.125 to 0.125
- old_logprob: float32 [16, 512], P('fsdp', 'seq'), may hold values from -0.15 to 0.15
- lengths: int32 [16, 4], P('fsdp', 'seq'), may hold values from 112 to 128
- rewards: float32 [16, 4], P('fsdp', 'seq'), may hold values from -5 to 5
- prompt_ids: int32 [16, 4], P('fsdp', 'seq'), may hold values from 0 to 3, as said below
- placement: int32 [16, 4], P('fsdp', 'seq'), may hold values from 0 to 15, as said below
Outputs:
- grad_context: bfloat16 [16, 512, 2560], P('fsdp', 'seq')
- grad_weight: float32 [2560, 2560], P('fsdp')
- loss: float32 [], replicated
Inputs may be any that keep to these rules, and one draw needn't show every extreme that they name: `prompt_ids`: every prompt id names exactly 16 rows. Sampler row (a, s) goes to learner row (placement[a, s], s) and keeps a mod 2; the 2 rows of one device go to 2 different fsdp indices; every learner row receives exactly one row; in every column one of the 2 rows of each device goes 8 / 2 fsdp indices onward and another goes 1 index onward, counted round.
All inputs are finite; a program needn't handle non-finite values.
Results may differ from a plain program's by a relative error of at most 0.014.
Values may be sent and summed in bfloat16 or wider, within the bound.
A program may use at most 128 MiB of HBM per device.

v0:
```python
import math
import jax
import jax.numpy as jnp
from jax import lax
from jax.sharding import PartitionSpec as P

DW = 2560
AW = 2560
GS = 16


def body(
    context,
    residual,
    target_rows,
    log_norm,
    norm_gain,
    out_proj,
    old_logprob,
    lengths,
    rewards,
    prompt_ids,
    placement,
):
    nrows = context.shape[0]
    lmax = context.shape[1]
    fsdp_ways = lax.axis_size("fsdp")
    seq_ways = lax.axis_size("seq")
    prompts = nrows * fsdp_ways * seq_ways // GS
    all_tokens = nrows * lmax * fsdp_ways * seq_ways
    reward_flat = rewards.reshape(-1)
    prompt_flat = prompt_ids.reshape(-1)
    length_flat = lengths.reshape(-1)
    dest_flat = placement.reshape(-1)
    prompt_range = jnp.arange(prompts, dtype=jnp.int32)
    local_hot = (prompt_flat[:, None] == prompt_range[None, :]).astype(jnp.float32)
    group_sum, group_sq, count = lax.psum(
        (
            jnp.sum(local_hot * reward_flat[:, None], axis=0),
            jnp.sum(local_hot * (reward_flat * reward_flat)[:, None], axis=0),
            jnp.sum(length_flat.astype(jnp.float32)),
        ),
        ("fsdp", "seq"),
    )
    group_mean = group_sum / GS
    group_var = group_sq / GS - group_mean * group_mean
    row_mean = jnp.sum(local_hot * group_mean[None, :], axis=1)
    row_var = jnp.sum(local_hot * group_var[None, :], axis=1)
    advantage = (reward_flat - row_mean) / jnp.sqrt(row_var + 0.25)
    slots = jnp.arange(nrows, dtype=jnp.int32)
    every_old, every_adv, every_len, every_dest = (
        lax.all_gather(old_logprob, "fsdp", axis=0, tiled=True),
        lax.all_gather(advantage, "fsdp", axis=0, tiled=True),
        lax.all_gather(length_flat, "fsdp", axis=0, tiled=True),
        lax.all_gather(dest_flat, "fsdp", axis=0, tiled=True),
    )
    wanted = lax.axis_index("fsdp") * nrows + slots
    chosen = every_dest[None, :] == wanted[:, None]
    learn_old = jnp.sum(jnp.where(chosen[:, :, None], every_old[None, :, :], 0.0), axis=1)
    learn_adv = jnp.sum(jnp.where(chosen, every_adv[None, :], 0.0), axis=1)
    learn_len = jnp.sum(jnp.where(chosen, every_len[None, :], 0), axis=1)
    offsets = jnp.arange(lmax, dtype=jnp.int32)
    valid = (offsets[None, :] < learn_len[:, None]).astype(jnp.float32).reshape(-1)
    token_adv = jnp.broadcast_to(learn_adv[:, None], (nrows, lmax)).reshape(-1)
    tokens = nrows * lmax
    context_flat = context.reshape(tokens, AW)
    whole = lax.all_gather(out_proj, "fsdp", axis=0, tiled=True)
    hidden = residual.reshape(tokens, DW).astype(jnp.float32) + jnp.dot(
        context_flat, whole, preferred_element_type=jnp.float32
    )
    rinv = lax.rsqrt(jnp.mean(hidden * hidden, axis=1) + 1e-06)
    vecs = norm_gain[None, :] * target_rows.reshape(tokens, DW).astype(jnp.float32)
    hv_sum = jnp.sum(hidden * vecs, axis=1)
    score = hv_sum * rinv
    ratio = jnp.exp(score - log_norm.reshape(-1) - learn_old.reshape(-1))
    plain = ratio * token_adv
    clipped = jnp.clip(ratio, 0.8, 1.2) * token_adv
    objective = jnp.minimum(plain, clipped)
    loss_local = jnp.sum(valid * -objective)
    dscore = -valid * jnp.where(plain <= clipped, plain, 0.0) / count
    dhid = (dscore * rinv)[:, None] * (vecs - hidden * (rinv * rinv * hv_sum / DW)[:, None])
    grad_hidden = (dhid * (32.0 * all_tokens * math.sqrt(DW))).astype(jnp.bfloat16)
    grad_context = lax.dot_general(
        grad_hidden, whole, (((1,), (1,)), ((), ())), preferred_element_type=jnp.float32
    ).astype(jnp.bfloat16)
    piece = lax.psum_scatter(
        lax.dot_general(
            context_flat, grad_hidden, (((0,), (0,)), ((), ())), preferred_element_type=jnp.float32
        ).astype(jnp.bfloat16),
        "fsdp",
        scatter_dimension=0,
        tiled=True,
    )
    grad_weight = lax.psum(piece, "seq").astype(jnp.float32) * (1.0 / math.sqrt(all_tokens))
    loss = lax.psum(loss_local, ("fsdp", "seq")) / count
    return (grad_context.reshape(nrows, lmax, AW), grad_weight, loss)


def solution(mesh):
    return jax.shard_map(
        body,
        mesh=mesh,
        in_specs=(
            P("fsdp", "seq", None),
            P("fsdp", "seq", None),
            P("fsdp", "seq", None),
            P("fsdp", "seq"),
            P(),
            P("fsdp", None),
            P("fsdp", "seq"),
            P("fsdp", "seq"),
            P("fsdp", "seq"),
            P("fsdp", "seq"),
            P("fsdp", "seq"),
        ),
        out_specs=(P("fsdp", "seq", None), P("fsdp", None), P()),
        check_vma=False,
    )
```

profile of v0, /device:TPU:0, one launch (start us, length us, event | category | flops | bytes accessed | tf_op | source)
XLA Modules:
  0.0 559.2 jit_solution(6872598172934750625)
XLA Ops:
  7.2 0.7 all-gather.5.cloned.1.call-update
  7.9 0.0 reduce-scatter.4.cloned.1.call-start
  8.0 0.7 multiply_bitcast_fusion
  8.6 0.8 select_reduce_fusion.6
  9.4 46.3 %all-reduce.5 = (f32[4]{0:T(128)S(1)}, f32[4]{0:T(128)S(1)}) all-reduce(f32[4]{0:T(128)S(1)} %get-tuple-element.16, f32[4]{0:T(128)S(1)} %get-tuple-element.17), channel_id=1, replica_groups=mesh['fsdp'=8,'seq'=4] {'fsdp','seq'}, use_global_device_ids=true, to_apply=%region_5.0 | all-reduce | flops 8 | bytes 64 | tf_op jit(solution)/shard_map/psum | solution.py:37
  55.7 1.2 dynamic-slice
  57.6 0.9 select_reduce_fusion.5
  58.5 0.8 bitcast_dynamic-update-slice_fusion.1
  59.2 0.7 multiply_dynamic-update-slice_fusion
  60.0 0.7 bitcast_dynamic-update-slice_fusion
  60.7 20.1 %all-reduce.2 = f32[16]{0:T(128)S(1)} all-reduce(f32[16]{0:T(128)S(1)} %multiply_dynamic-update-slice_fusion), channel_id=1, replica_groups=mesh['fsdp'=8,'seq'=4] {'fsdp'}, use_global_device_ids=true, to_apply=%add.2 | all-reduce | flops 16 | bytes 128
  80.9 12.8 %all-reduce.3 = (s32[16]{0:T(128)S(1)}, s32[16]{0:T(128)S(1)}) all-reduce(s32[16]{0:T(128)S(1)} %bitcast_dynamic-update-slice_fusion.1, s32[16]{0:T(128)S(1)} %bitcast_dynamic-update-slice_fusion), channel_id=2, replica_groups=mesh['fsdp'=8,'seq'=4] {'fsdp'}, use_global_device_ids=true, to_apply=%add | all-reduce | flops 32 | bytes 256
  93.7 18.2 %all-gather.2 = f32[8,2,128]{2,1,0:T(2,128)S(1)} all-gather(f32[1,2,128]{2,1,0:T(2,128)} %bitcast.68), channel_id=1, replica_groups=mesh['fsdp'=8,'seq'=4] {'fsdp'}, dimensions={0}, use_global_device_ids=true | all-gather | bytes 9216 | tf_op jit(solution)/shard_map/all_gather | solution.py:52
  111.9 1.3 convert_reduce_fusion
  113.1 0.2 select_reduce_fusion.2
  113.3 0.1 select_reduce_fusion.7
  113.4 0.1 select_reduce_fusion
  113.5 83.5 %all-gather.5.cloned.1.call-done = bf16[2560,2560]{1,0:T(8,128)(2,1)} async-done(((bf16[320,2560]{1,0:T(8,128)(2,1)}), bf16[2560,2560]{1,0:T(8,128)(2,1)}) %all-gather.5.cloned.1.call-update) | async-done | bytes 13107216 | tf_op jit(solution)/shard_map/all_gather | solution.py:67
  197.0 10.4 %multiply_reduce_fusion = (f32[256]{0:T(256)S(1)}, f32[256]{0:T(256)S(1)}, f32[256,2560]{1,0:T(8,128)}) fusion(bf16[2,128,2560]{2,1,0:T(8,128)(2,1)} %param.13, f32[2560]{0:T(1024)} %param.15, bf16[256,2560]{1,0:T(8,128)(2,1)S(1)} %bitcast.62, bf16[2560,2560]{1,0:T(8,128)(2,1)} %all-gather.5.cloned.1.call-done, bf16[256,2560]{1,0:T(8,128)(2,1)} %bitcast.69), kind=kOutput, calls=%fused_computation.12 | convolution fusion | flops 3360685568 | bytes 19673088 | tf_op jit(solution)/shard_map/dot_general | solution.py:68
  207.4 0.7 select_reduce_fusion.1
  208.1 38.7 %all-reduce.4 = (f32[]{:T(128)}, f32[]{:T(128)}) all-reduce(f32[]{:T(128)} %convert_reduce_fusion, f32[]{:T(128)} %select_reduce_fusion.1), channel_id=1, replica_groups=mesh['fsdp'=8,'seq'=4] {'fsdp','seq'}, use_global_device_ids=true, to_apply=%region_12.13 | all-reduce | flops 2 | bytes 16 | tf_op jit(solution)/shard_map/psum | solution.py:37
  246.7 0.7 divide_multiply_fusion
  247.5 2.7 fusion.6
  250.2 6.8 %fusion = bf16[2560,2560]{0,1:T(8,128)(2,1)} fusion(bf16[256,2560]{1,0:T(8,128)(2,1)S(1)} %fusion.6, bf16[256,2560]{1,0:T(8,128)(2,1)S(1)} %bitcast.63), kind=kOutput, calls=%fused_computation.1 | convolution fusion | flops 3361996800 | bytes 15728640 | tf_op jit(solution)/shard_map/dot_general | solution.py:87
  257.0 17.6 %copy.17 = bf16[2560,2560]{1,0:T(8,128)(2,1)} copy(bf16[2560,2560]{0,1:T(8,128)(2,1)} %fusion) | data formatting | bytes 26214400
  274.6 0.0 all-reduce.8.cloned.1.call-start
  276.0 214.2 %reduce-scatter.4.cloned.1.call-done = bf16[320,2560]{1,0:T(8,128)(2,1)} async-done(((bf16[2560,2560]{1,0:T(8,128)(2,1)}), bf16[320,2560]{1,0:T(8,128)(2,1)}) %reduce-scatter.4.cloned.1.call-update) | async-done | bytes 1638416
  490.2 3.8 copy.18
  494.0 9.4 %convolution_convert_fusion.1 = bf16[256,2560]{1,0:T(8,128)(2,1)} fusion(bf16[256,2560]{1,0:T(8,128)(2,1)S(1)} %fusion.6, bf16[2560,2560]{1,0:T(8,128)(2,1)} %all-gather.5.cloned.1.call-done), kind=kOutput, calls=%fused_computation.4 | convolution fusion | flops 3356098560 | bytes 15728640 | tf_op jit(solution)/shard_map/dot_general | solution.py:83
  503.4 39.1 %all-reduce.8.cloned.1.call-done = bf16[320,2560]{0,1:T(8,128)(2,1)} async-done(((bf16[320,2560]{0,1:T(8,128)(2,1)}), bf16[320,2560]{0,1:T(8,128)(2,1)}) %all-reduce.8.cloned.1.call-update) | async-done | bytes 1638416 | tf_op jit(solution)/shard_map/psum | solution.py:94
  542.6 3.8 convert_multiply_fusion
  546.3 5.2 copy.16
  (14 shorter events, 0.1 us)
Async XLA Ops:
  7.2 189.9 %copy-start = (bf16[2,128,2560]{2,1,0:T(8,128)(2,1)S(1)}, bf16[2,128,2560]{2,1,0:T(8,128)(2,1)}, u32[]{:S(2)}) copy-start(bf16[2,128,2560]{2,1,0:T(8,128)(2,1)} %param.11) | copy-start | bytes 3932164
  7.2 189.9 %all-gather.5.cloned.1.call-start = ((), (), s32[]{:S(2)}) async-start(), calls=%async_computation.1 | async-start | bytes 14745600 | tf_op jit(solution)/shard_map/all_gather | solution.py:67
  7.9 482.3 %reduce-scatter.4.cloned.1.call-start = ((), (), s32[]{:S(2)}) async-start(), calls=%async_computation.3 | async-start | bytes 14745600
  197.0 10.4 %copy-start.2 = (f32[2,128]{1,0:T(2,128)S(1)}, f32[2,128]{1,0:T(2,128)}, u32[]{:S(2)}) copy-start(f32[2,128]{1,0:T(2,128)} %param.14) | copy-start | bytes 3076
  197.0 50.4 %copy-start.1 = (f32[2560]{0:T(1024)S(1)}, f32[2560]{0:T(1024)}, u32[]{:S(2)}) copy-start(f32[2560]{0:T(1024)} %param.15) | copy-start | bytes 30724
  274.6 267.9 %all-reduce.8.cloned.1.call-start = ((), (), s32[]{:S(2)}) async-start(), calls=%async_computation.2 | async-start | bytes 3932160 | tf_op jit(solution)/shard_map/psum | solution.py:94
Sparse Core Ops, SparseCore 0:
  10.2 186.7 all-gather.4
  274.7 215.4 reduce-scatter.3
  494.2 48.3 all-reduce.7
where the time goes:
time: 560 us; the launch traced here: 559 us
  waiting for transfers between devices  338 us (60%)
  blocking collectives  136 us (24%)
  local copies, waits for them, and re-layouts  29.4 us (5%)
  matrix products  26.5 us (5%)
  between operations  16.9 us (3%)
  other arithmetic  12.6 us (2%)
    unnamed x4, waiting for transfers between devices  215 us
    psum x2, blocking collectives, body(): lax.psum((jnp.sum(local_hot * reward_flat[:, None], axis=0), jnp.sum(loca...  85 us
    all_gather x1, waiting for transfers between devices, body(): whole = lax.all_gather(out_proj, 'fsdp', axis=0, tiled=True)  83.5 us
    psum x1, waiting for transfers between devices, body(): lax.psum(piece, 'seq').astype(jnp.float32) * (1.0 / math.sqrt(all_tokens))  39.1 us
    unnamed x2, blocking collectives  33 us
    unnamed x15, local copies, waits for them, and re-layouts  29.4 us
    all_gather x1, blocking collectives, body(): lax.all_gather(old_logprob, 'fsdp', axis=0, tiled=True)  18.2 us
  transfers between devices with their start and end apart: 3, of which 3 were waited for; matrix products, arithmetic and copies ran while one was open for 3% of the time, Pallas kernels for 0%

commit v1 on v0

--- a/solution.py
+++ b/solution.py
@@ -7,6 +7,13 @@
 DW = 2560
 AW = 2560
 GS = 16
+
+
+def swapped_in(x, mesh_axis, dim):
+    count = lax.axis_size(mesh_axis)
+    blocks = jnp.stack([x for _ in range(count)])
+    blocks = lax.all_to_all(blocks, mesh_axis, split_axis=0, concat_axis=0)
+    return jnp.concatenate(blocks, axis=dim)
 
 
 def body(
@@ -49,7 +56,7 @@
     advantage = (reward_flat - row_mean) / jnp.sqrt(row_var + 0.25)
     slots = jnp.arange(nrows, dtype=jnp.int32)
     every_old, every_adv, every_len, every_dest = (
-        lax.all_gather(old_logprob, "fsdp", axis=0, tiled=True),
+        swapped_in(old_logprob, "fsdp", 0),
         lax.all_gather(advantage, "fsdp", axis=0, tiled=True),
         lax.all_gather(length_flat, "fsdp", axis=0, tiled=True),
         lax.all_gather(dest_flat, "fsdp", axis=0, tiled=True),

time: 560 us -> 560 us (level)
  blocking collectives: 136 us -> 111 us
  waiting for transfers between devices: 338 us -> 354 us
  starting transfers between devices: 0.12 us -> 7.37 us
    all_gather x1 -> x0, blocking collectives: 18.2 us -> none  [body(): lax.all_gather(old_logprob, 'fsdp', axis=0, tiled=True)]
    all_gather x1, waiting for transfers between devices: 83.5 us -> 100 us  [body(): whole = lax.all_gather(out_proj, 'fsdp', axis=0, tiled=True)]
    all_to_all x0 -> x1, starting transfers between devices: none -> 7.25 us  [swapped_in(): blocks = lax.all_to_all(blocks, mesh_axis, split_axis=0, concat_axis=0)]
    unnamed x2, blocking collectives: 33 us -> 26.7 us
  transfers between devices with their start and end apart: 3 -> 4, of which waited for: 3 -> 3; matrix products, arithmetic and copies ran while one was open for 3% -> 3% of each run, Pallas kernels for 0% -> 0%
where the time goes in v1:
time: 560 us; the launch traced here: 559 us
  waiting for transfers between devices  354 us (63%)
  blocking collectives  111 us (20%)
  local copies, waits for them, and re-layouts  30.7 us (5%)
  matrix products  26.6 us (5%)
  between operations  16.9 us (3%)
  other arithmetic  12.6 us (2%)
  starting transfers between devices  7.37 us (1%)
    unnamed x4, waiting for transfers between devices  215 us
    all_gather x1, waiting for transfers between devices, body(): whole = lax.all_gather(out_proj, 'fsdp', axis=0, tiled=True)  100 us
    psum x2, blocking collectives, body(): lax.psum((jnp.sum(local_hot * reward_flat[:, None], axis=0), jnp.sum(loca...  84.2 us
    psum x1, waiting for transfers between devices, body(): lax.psum(piece, 'seq').astype(jnp.float32) * (1.0 / math.sqrt(all_tokens))  39.1 us
    unnamed x15, local copies, waits for them, and re-layouts  29.4 us
    unnamed x2, blocking collectives  26.7 us
  transfers between devices with their start and end apart: 4, of which 3 were waited for; matrix products, arithmetic and copies ran while one was open for 3% of the time, Pallas kernels for 0%

profile of v1, /device:TPU:0, one launch (start us, length us, event | category | flops | bytes accessed | tf_op | source)
XLA Modules:
  0.0 559.1 jit_solution(15463113069425308905)
XLA Ops:
  7.2 0.7 all-gather.4.cloned.1.call-update
  7.9 1.3 stack.2
  9.2 7.3 %all-to-all-start = ((f32[8,2,128]{2,1,0:T(2,128)}), f32[8,2,128]{2,1,0:T(2,128)S(1)}, u32[]{:S(2)}, u32[]{:S(2)}) async-start(f32[8,2,128]{2,1,0:T(2,128)} %stack.2), calls=%async_computation | async-start | bytes 16384 | tf_op jit(solution)/shard_map/all_to_all | solution.py:15
  16.5 0.7 multiply_bitcast_fusion
  17.2 0.8 select_reduce_fusion.6
  17.9 45.5 %all-reduce.5 = (f32[4]{0:T(128)S(1)}, f32[4]{0:T(128)S(1)}) all-reduce(f32[4]{0:T(128)S(1)} %get-tuple-element.16, f32[4]{0:T(128)S(1)} %get-tuple-element.17), channel_id=1, replica_groups=mesh['fsdp'=8,'seq'=4] {'fsdp','seq'}, use_global_device_ids=true, to_apply=%region_5.0 | all-reduce | flops 8 | bytes 64 | tf_op jit(solution)/shard_map/psum | solution.py:44
  63.4 1.2 dynamic-slice
  65.3 0.9 select_reduce_fusion.5
  66.2 0.8 bitcast_dynamic-update-slice_fusion.1
  66.9 0.7 multiply_dynamic-update-slice_fusion
  67.7 0.7 bitcast_dynamic-update-slice_fusion
  68.4 19.9 %all-reduce.2 = f32[16]{0:T(128)S(1)} all-reduce(f32[16]{0:T(128)S(1)} %multiply_dynamic-update-slice_fusion), channel_id=1, replica_groups=mesh['fsdp'=8,'seq'=4] {'fsdp'}, use_global_device_ids=true, to_apply=%add.2 | all-reduce | flops 16 | bytes 128
  88.4 6.8 %all-reduce.3 = (s32[16]{0:T(128)S(1)}, s32[16]{0:T(128)S(1)}) all-reduce(s32[16]{0:T(128)S(1)} %bitcast_dynamic-update-slice_fusion.1, s32[16]{0:T(128)S(1)} %bitcast_dynamic-update-slice_fusion), channel_id=2, replica_groups=mesh['fsdp'=8,'seq'=4] {'fsdp'}, use_global_device_ids=true, to_apply=%add | all-reduce | flops 32 | bytes 256
  95.2 0.2 select_reduce_fusion.2
  95.3 0.1 select_reduce_fusion.7
  95.5 1.3 convert_reduce_fusion
  96.7 0.1 select_reduce_fusion
  96.8 100.1 %all-gather.4.cloned.1.call-done = bf16[2560,2560]{1,0:T(8,128)(2,1)} async-done(((bf16[320,2560]{1,0:T(8,128)(2,1)}), bf16[2560,2560]{1,0:T(8,128)(2,1)}) %all-gather.4.cloned.1.call-update) | async-done | bytes 13107216 | tf_op jit(solution)/shard_map/all_gather | solution.py:74
  196.9 10.4 %multiply_reduce_fusion = (f32[256]{0:T(256)S(1)}, f32[256]{0:T(256)S(1)}, f32[256,2560]{1,0:T(8,128)}) fusion(bf16[2,128,2560]{2,1,0:T(8,128)(2,1)} %param.13, f32[2560]{0:T(1024)} %param.15, bf16[256,2560]{1,0:T(8,128)(2,1)S(1)} %bitcast.61, bf16[2560,2560]{1,0:T(8,128)(2,1)} %all-gather.4.cloned.1.call-done, bf16[256,2560]{1,0:T(8,128)(2,1)} %bitcast.67), kind=kOutput, calls=%fused_computation.12 | convolution fusion | flops 3360685568 | bytes 19673088 | tf_op jit(solution)/shard_map/dot_general | solution.py:75
  207.3 0.7 select_reduce_fusion.1
  207.9 38.7 %all-reduce.4 = (f32[]{:T(128)}, f32[]{:T(128)}) all-reduce(f32[]{:T(128)} %convert_reduce_fusion, f32[]{:T(128)} %select_reduce_fusion.1), channel_id=1, replica_groups=mesh['fsdp'=8,'seq'=4] {'fsdp','seq'}, use_global_device_ids=true, to_apply=%region_12.13 | all-reduce | flops 2 | bytes 16 | tf_op jit(solution)/shard_map/psum | solution.py:44
  246.6 0.7 divide_multiply_fusion
  247.3 2.7 fusion.6
  250.1 6.8 %fusion = bf16[2560,2560]{0,1:T(8,128)(2,1)} fusion(bf16[256,2560]{1,0:T(8,128)(2,1)S(1)} %fusion.6, bf16[256,2560]{1,0:T(8,128)(2,1)S(1)} %bitcast.62), kind=kOutput, calls=%fused_computation.1 | convolution fusion | flops 3361996800 | bytes 15728640 | tf_op jit(solution)/shard_map/dot_general | solution.py:94
  256.8 17.6 %copy.17 = bf16[2560,2560]{1,0:T(8,128)(2,1)} copy(bf16[2560,2560]{0,1:T(8,128)(2,1)} %fusion) | data formatting | bytes 26214400
  274.5 0.0 all-reduce.8.cloned.1.call-start
  275.9 214.3 %reduce-scatter.4.cloned.1.call-done = bf16[320,2560]{1,0:T(8,128)(2,1)} async-done(((bf16[2560,2560]{1,0:T(8,128)(2,1)}), bf16[320,2560]{1,0:T(8,128)(2,1)}) %reduce-scatter.4.cloned.1.call-update) | async-done | bytes 1638416
  490.1 3.8 copy.18
  494.0 9.4 %convolution_convert_fusion.1 = bf16[256,2560]{1,0:T(8,128)(2,1)} fusion(bf16[256,2560]{1,0:T(8,128)(2,1)S(1)} %fusion.6, bf16[2560,2560]{1,0:T(8,128)(2,1)} %all-gather.4.cloned.1.call-done), kind=kOutput, calls=%fused_computation.4 | convolution fusion | flops 3356098560 | bytes 15728640 | tf_op jit(solution)/shard_map/dot_general | solution.py:90
  503.4 39.1 %all-reduce.8.cloned.1.call-done = bf16[320,2560]{0,1:T(8,128)(2,1)} async-done(((bf16[320,2560]{0,1:T(8,128)(2,1)}), bf16[320,2560]{0,1:T(8,128)(2,1)}) %all-reduce.8.cloned.1.call-update) | async-done | bytes 1638416 | tf_op jit(solution)/shard_map/psum | solution.py:101
  542.5 3.8 convert_multiply_fusion
  546.2 5.2 copy.16
  (16 shorter events, 0.1 us)
Async XLA Ops:
  7.2 189.7 %copy-start = (bf16[2,128,2560]{2,1,0:T(8,128)(2,1)S(1)}, bf16[2,128,2560]{2,1,0:T(8,128)(2,1)}, u32[]{:S(2)}) copy-start(bf16[2,128,2560]{2,1,0:T(8,128)(2,1)} %param.11) | copy-start | bytes 3932164
  7.2 189.7 %all-gather.4.cloned.1.call-start = ((), (), s32[]{:S(2)}) async-start(), calls=%async_computation.2 | async-start | bytes 14745600 | tf_op jit(solution)/shard_map/all_gather | solution.py:74
  9.2 87.5 %all-to-all-start = ((f32[8,2,128]{2,1,0:T(2,128)}), f32[8,2,128]{2,1,0:T(2,128)S(1)}, u32[]{:S(2)}, u32[]{:S(2)}) async-start(f32[8,2,128]{2,1,0:T(2,128)} %stack.2), calls=%async_computation | async-start | bytes 16384 | tf_op jit(solution)/shard_map/all_to_all | solution.py:15
  16.4 473.7 %reduce-scatter.4.cloned.1.call-start = ((), (), s32[]{:S(2)}) async-start(), calls=%async_computation.4 | async-start | bytes 14745600
  196.9 10.4 %copy-start.2 = (f32[2,128]{1,0:T(2,128)S(1)}, f32[2,128]{1,0:T(2,128)}, u32[]{:S(2)}) copy-start(f32[2,128]{1,0:T(2,128)} %param.14) | copy-start | bytes 3076
  196.9 50.4 %copy-start.1 = (f32[2560]{0:T(1024)S(1)}, f32[2560]{0:T(1024)}, u32[]{:S(2)}) copy-start(f32[2560]{0:T(1024)} %param.15) | copy-start | bytes 30724
  274.5 268.0 %all-reduce.8.cloned.1.call-start = ((), (), s32[]{:S(2)}) async-start(), calls=%async_computation.3 | async-start | bytes 3932160 | tf_op jit(solution)/shard_map/psum | solution.py:101
Sparse Core Ops, SparseCore 0:
  10.2 186.6 all-gather.3
  274.6 215.4 reduce-scatter.3
  494.1 48.3 all-reduce.7
